TPU v7x, 32 devices: a whole 2x2x4 slice. The times are simulated.
32 devices in a mesh: wide: 8 (over z, y), narrow: 4 (over x, core).
Axes of the slice: x: 2, y: 2, z: 4, core: 2. Of those that a mesh axis runs over, the one named last changes fastest.
Arguments:
- residual: float32 [8, 4, 6, 192, 512], P('wide', 'narrow'), may hold values from -6 to 6
- face_schur: float32 [8, 4, 6, 192, 192], P('wide', 'narrow'), may hold values from -0.5 to 1.5, as said below
- local_solver: bfloat16 [8, 4, 1152, 1152], P('wide', 'narrow'), may hold values from -0.1875 to 0.1875
- interface_functional_set: float32 [3, 192, 16], replicated, may hold values from -0.4375 to 0.4375
- coarse_inverse: float32 [1536, 1536], P('wide', 'narrow'), may hold values from -0.3125 to 0.3125
Outputs:
- preconditioned: float32 [8, 4, 3, 192, 512], P('wide', 'narrow')
Inputs may be any that keep to these rules, and one draw needn't show every extreme that they name: `face_schur`: every face block is symmetric positive definite.
All inputs are finite; a program needn't handle non-finite values. Where the computation divides by a largest or mean magnitude, that divisor is 1e-20 or more.
Results may differ from a plain program's by a relative error of at most 0.002.
Values sent between devices are 32-bit elements; how exact they have to be, the bound alone decides.
No kernel may reach another device: no remote copies, remote signals or barrier semaphores. Data moves between devices by JAX's collectives and lax.ppermute only.
A program may use at most 64 MiB of HBM per device.

v0:
```python
import jax
import jax.numpy as jnp
from jax import lax
from jax.sharding import PartitionSpec as P

NS_STEPS = 12
exact_arithmetic_mode = lax.Precision.HIGHEST


def passed_along(value, axis, steps):
    count = lax.axis_size(axis)
    pairs = [(source, (source + steps) % count) for source in range(count)]
    return lax.ppermute(value, axis, pairs)


def newton_schulz(matrices):
    row_sums = jnp.max(jnp.sum(jnp.abs(matrices), axis=2), axis=1)
    approx = matrices / (row_sums * row_sums)[:, None, None]
    for iteration in range(NS_STEPS):
        product = jnp.einsum("bij,bjk->bik", matrices, approx, precision=exact_arithmetic_mode)
        approx = 2.0 * approx - jnp.einsum(
            "bij,bjk->bik", approx, product, precision=exact_arithmetic_mode
        )
    return approx


def apply_faces(blocks, fields):
    return jnp.einsum("fij,fjr->fir", blocks, fields, precision=exact_arithmetic_mode)


def per_device(residual, face_schur, local_solver, interface_functional_set, coarse_inverse):
    blocks = face_schur[0, 0]
    face_loads = residual[0, 0]
    face_order = blocks.shape[1]
    columns_count = face_loads.shape[2]
    wide_low = jnp.concatenate([blocks[0], face_loads[0]], axis=1)
    wide_above = passed_along(wide_low, "wide", -1)
    narrow_low = jnp.concatenate([blocks[2], face_loads[2]], axis=1)
    narrow_above = passed_along(narrow_low, "narrow", -1)
    owned_sums = jnp.stack(
        [
            blocks[1] + wide_above[:, :face_order],
            blocks[3] + narrow_above[:, :face_order],
            blocks[4] + blocks[5],
        ],
        axis=0,
    )
    owned_values = jnp.stack(
        [
            face_loads[1] + wide_above[:, face_order:],
            face_loads[3] + narrow_above[:, face_order:],
            face_loads[4] + face_loads[5],
        ],
        axis=0,
    )
    owned_inverse = newton_schulz(owned_sums)
    owned_scaled = apply_faces(owned_inverse, owned_values)
    wide_below = passed_along(owned_scaled[0], "wide", 1)
    narrow_below = passed_along(owned_scaled[1], "narrow", 1)
    face_scaled = jnp.stack(
        [
            wide_below,
            owned_scaled[0],
            narrow_below,
            owned_scaled[1],
            owned_scaled[2],
            owned_scaled[2],
        ],
        axis=0,
    )
    restricted_residual = jnp.einsum(
        "psk,pse->pke", interface_functional_set, owned_values, precision=exact_arithmetic_mode
    )
    restricted_residual = restricted_residual.reshape(-1, columns_count)
    incomplete_total = jnp.dot(
        coarse_inverse,
        lax.all_gather(restricted_residual, "wide", axis=0, tiled=True),
        precision=exact_arithmetic_mode,
        preferred_element_type=jnp.float32,
    )
    own_rows = restricted_residual.shape[0]
    summed = lax.psum(incomplete_total, "narrow")
    own_coarse = lax.dynamic_slice_in_dim(summed, lax.axis_index("narrow") * own_rows, own_rows, 0)
    local_loads = apply_faces(blocks, face_scaled).astype(jnp.bfloat16)
    flattened = local_loads.reshape(-1, columns_count)
    solved = jnp.dot(local_solver[0, 0], flattened, preferred_element_type=jnp.float32)
    solved = solved.reshape(6, face_order, columns_count)
    weighted = apply_faces(blocks, solved)
    wide_back = passed_along(weighted[0], "wide", -1)
    narrow_back = passed_along(weighted[2], "narrow", -1)
    combined = jnp.stack(
        [weighted[1] + wide_back, weighted[3] + narrow_back, weighted[4] + weighted[5]], axis=0
    )
    local_part = apply_faces(owned_inverse, combined)
    update_increment = own_coarse.reshape(3, -1, columns_count)
    coarse_component = jnp.einsum(
        "fek,fkg->feg", interface_functional_set, update_increment, precision=exact_arithmetic_mode
    )
    output_answer = local_part + coarse_component
    return output_answer[None, None]


def solution(mesh):
    placed = (
        P("wide", "narrow", None, None, None),
        P("wide", "narrow", None, None, None),
        P("wide", "narrow", None, None),
        P(),
        P("wide", "narrow"),
    )
    return jax.shard_map(
        per_device,
        mesh=mesh,
        in_specs=placed,
        out_specs=P("wide", "narrow", None, None, None),
        check_vma=False,
    )
```

profile of v0, /device:TPU:0, one launch (start us, length us, event | category | flops | bytes accessed | tf_op | source)
XLA Modules:
  0.0 147.2 jit_solution(12711466252790806071)
XLA Ops:
  6.5 1.4 add_bitcast_fusion.1
  8.0 2.3 %slice_bitcast_fusion.6 = (f32[192,512]{1,0:T(8,128)S(1)}, f32[192,512]{1,0:T(8,128)S(1)}, f32[1,192,512]{2,1,0:T(8,128)}) fusion(f32[1,1,6,192,512]{4,3,2,1,0:T(8,128)} %param.5), kind=kLoop, calls=%fused_computation.57 | loop fusion | flops 98304 | bytes 2752512 | tf_op jit(solution)/shard_map/squeeze | solution.py:36
  10.4 2.5 %collective-permute-start.1 = (f32[192,704]{1,0:T(8,128)S(1)}, f32[192,704]{1,0:T(8,128)S(1)}, u32[]{:S(2)}, u32[]{:S(2)}) collective-permute-start(f32[192,704]{1,0:T(8,128)S(1)} %pad_maximum_fusion.4), channel_id=1, source_target_pairs={{0,3},{1,0},{2,1},{3,2},{4,7},{5,4},{6,5},{7,6},{8,11},{9,8},{10,9... | collective-permute-start | bytes 1622024 | tf_op jit(solution)/shard_map/ppermute | solution.py:13
  13.1 4.6 %collective-permute-start = (f32[192,704]{1,0:T(8,128)S(1)}, f32[192,704]{1,0:T(8,128)S(1)}, u32[]{:S(2)}, u32[]{:S(2)}) collective-permute-start(f32[192,704]{1,0:T(8,128)S(1)} %pad_maximum_fusion.3), channel_id=1, source_target_pairs={{0,28},{4,0},{8,4},{12,8},{16,12},{20,16},{24,20},{28,24},{1,29},{... | collective-permute-start | bytes 1622024 | tf_op jit(solution)/shard_map/ppermute | solution.py:13
  17.7 2.6 %collective-permute-done.1 = f32[192,704]{1,0:T(8,128)S(1)} collective-permute-done((f32[192,704]{1,0:T(8,128)S(1)}, f32[192,704]{1,0:T(8,128)S(1)}, u32[]{:S(2)}, u32[]{:S(2)}) %collective-permute-start.1) | collective-permute-done | bytes 540704 | tf_op jit(solution)/shard_map/ppermute | solution.py:13
  20.3 9.7 %collective-permute-done = f32[192,704]{1,0:T(8,128)S(1)} collective-permute-done((f32[192,704]{1,0:T(8,128)S(1)}, f32[192,704]{1,0:T(8,128)S(1)}, u32[]{:S(2)}, u32[]{:S(2)}) %collective-permute-start) | collective-permute-done | bytes 540704 | tf_op jit(solution)/shard_map/ppermute | solution.py:13
  30.0 1.3 fusion.23
  31.6 0.8 fusion.11
  32.4 0.8 convolution_subtract_fusion.11
  33.2 0.7 fusion.37
  33.9 0.7 convolution_subtract_fusion.10
  34.7 0.7 fusion.36
  35.4 0.7 convolution_subtract_fusion.9
  36.1 0.7 fusion.35
  36.8 0.7 convolution_subtract_fusion.8
  37.6 0.7 fusion.34
  38.3 0.7 convolution_subtract_fusion.7
  39.0 0.7 fusion.33
  39.7 0.7 convolution_subtract_fusion.6
  40.5 0.7 fusion.32
  41.2 0.7 convolution_subtract_fusion.5
  41.9 0.7 fusion.31
  43.4 0.9 fusion.30
  45.0 0.7 fusion.29
  46.4 0.7 fusion.28
  47.9 0.7 fusion.27
  49.9 1.4 fusion.19
  51.3 1.2 fusion.10
  52.9 0.7 fusion.9
  53.6 12.1 %collective-permute-done.2 = f32[192,512]{1,0:T(8,128)S(1)} collective-permute-done((f32[192,512]{1,0:T(8,128)S(1)}, f32[192,512]{1,0:T(8,128)S(1)}, u32[]{:S(2)}, u32[]{:S(2)}) %collective-permute-start.2) | collective-permute-done | bytes 393248 | tf_op jit(solution)/shard_map/ppermute | solution.py:13
  65.8 0.8 slice_bitcast_fusion.4
  66.6 1.4 copy-done.4
  68.0 32.6 %all_gather.3 = f32[384,512]{1,0:T(8,128)S(1)} all-gather(f32[48,512]{1,0:T(8,128)S(1)} %bitcast.129), channel_id=1, replica_groups=mesh['wide'=8,'narrow'=4] {'wide'}, dimensions={0}, use_global_device_ids=true | all-gather | bytes 884736 | tf_op jit(solution)/shard_map/all_gather | solution.py:77
  100.6 1.6 %convolution_bitcast_fusion.3 = f32[192,512]{1,0:T(8,128)} fusion(f32[384,512]{1,0:T(8,128)S(1)} %all_gather.3, f32[192,384]{1,0:T(8,128)S(1)} %copy-done.11), kind=kOutput, calls=%fused_computation.19 | convolution fusion | flops 452984832 | bytes 1474560 | tf_op jit(solution)/shard_map/dot_general | solution.py:75
  102.3 1.8 %bitcast_dynamic-update-slice_fusion = f32[6,192,512]{2,1,0:T(8,128)} fusion(f32[6,192,512]{2,1,0:T(8,128)} %copy-done.4, f32[192,512]{1,0:T(8,128)} %collective-permute-done.3), kind=kLoop, calls=%fused_computation.53 | loop fusion | bytes 786432
  104.1 2.2 %slice_dynamic-update-slice_fusion = f32[6,192,512]{2,1,0:T(8,128)} fusion(f32[6,192,512]{2,1,0:T(8,128)} %bitcast_dynamic-update-slice_fusion, f32[3,192,512]{2,1,0:T(8,128)} %copy-done.1), kind=kLoop, calls=%fused_computation.30 | loop fusion | bytes 1572864
  106.2 1.8 %slice_dynamic-update-slice_fusion.1 = f32[6,192,512]{2,1,0:T(8,128)} fusion(f32[6,192,512]{2,1,0:T(8,128)} %slice_dynamic-update-slice_fusion, f32[3,192,512]{2,1,0:T(8,128)} %copy-done.1), kind=kLoop, calls=%fused_computation.47 | loop fusion | bytes 786432 | tf_op jit(solution)/shard_map/stack | solution.py:60
  108.0 4.0 %convolution_convert_fusion = bf16[6,512,192]{1,2,0:T(8,128)(2,1)S(1)} fusion(f32[6,192,512]{2,1,0:T(8,128)} %slice_dynamic-update-slice_fusion.1, f32[1,1,6,192,192]{4,3,2,1,0:T(8,128)S(1)} %copy-done.2), kind=kOutput, calls=%fused_computation.3 | convolution fusion | flops 1359544320 | bytes 4423680 | tf_op jit(solution)/shard_map/fij,fjr->fir/dot_general | solution.py:28
  112.0 3.4 %convolution_bitcast_fusion = f32[1152,512]{0,1:T(8,128)} fusion(bf16[1152,512]{1,0:T(8,128)(2,1)S(1)} %bitcast.127, bf16[1,1,1152,1152]{3,2,1,0:T(8,128)(2,1)S(1)} %copy-done), kind=kOutput, calls=%fused_computation | convolution fusion | flops 1358954496 | bytes 6193152 | tf_op jit(solution)/shard_map/dot_general | solution.py:86
  115.4 3.1 %copy.8 = f32[1152,512]{1,0:T(8,128)} copy(f32[1152,512]{0,1:T(8,128)} %convolution_bitcast_fusion) | data formatting | bytes 4718592 | tf_op jit(solution)/shard_map/dot_general | solution.py:86
  118.5 4.3 %convolution_bitcast_fusion.1 = f32[6,192,512]{2,1,0:T(8,128)S(1)} fusion(f32[6,192,512]{2,1,0:T(8,128)} %bitcast.126, f32[1,1,6,192,192]{4,3,2,1,0:T(8,128)} %param.6), kind=kOutput, calls=%fused_computation.2 | convolution fusion | flops 1358954496 | bytes 5603328 | tf_op jit(solution)/shard_map/fij,fjr->fir/dot_general | solution.py:28
  122.8 1.1 slice_bitcast_fusion.2
  124.6 1.4 collective-permute-start.4
  126.0 8.5 %all-reduce.2.cloned.1.call-done = f32[192,512]{1,0:T(8,128)} async-done(((f32[192,512]{1,0:T(8,128)}), f32[192,512]{1,0:T(8,128)}) %all-reduce.2.cloned.1.call-update) | async-done | bytes 393232 | tf_op jit(solution)/shard_map/psum | solution.py:82
  134.5 0.9 constant_dynamic-slice_fusion
  135.4 1.1 convolution_bitcast_fusion.2
  136.6 1.5 %fusion.17 = (f32[1,192,512]{2,1,0:T(8,128)S(1)}, f32[1,192,512]{2,1,0:T(8,128)S(1)}) fusion(f32[192,512]{1,0:T(8,128)} %collective-permute-done.4, f32[6,192,512]{2,1,0:T(8,128)} %copy-done.3, f32[192,512]{1,0:T(8,128)} %collective-permute-done.5), kind=kLoop, calls=%fused_computation.46 | loop fusion | flops 196608 | bytes 2359296 | tf_op jit(solution)/shard_map/stack | solution.py:91
  138.1 2.2 %fusion.1 = f32[1,1,3,192,512]{4,3,2,1,0:T(8,128)} fusion(f32[3,192,512]{2,1,0:T(8,128)S(1)} %convolution_bitcast_fusion.2, f32[3,192,192]{2,1,0:T(8,128)S(1)} %convolution_subtract_fusion, f32[1,192,512]{2,1,0:T(8,128)S(1)} %copy-done.6, f32[1,192,512]{2,1,0:T(8,128)S(1)} %get-tuple-element.6, f32[1,192,512]{2,1,0:T(8,128)S(1)} %get-tuple-element.5), kind=kOutput, calls=%fused_computation.6 | convolution fusion | flops 680361984 | bytes 3981312 | tf_op jit(solution)/shard_map/fij,fjr->fir/dot_general | solution.py:28
  (45 shorter events, 5.9 us)
Async XLA Ops:
  6.5 105.5 %copy-start = (bf16[1,1,1152,1152]{3,2,1,0:T(8,128)(2,1)S(1)}, bf16[1,1,1152,1152]{3,2,1,0:T(8,128)(2,1)}, u32[]{:S(2)}) copy-start(bf16[1,1,1152,1152]{3,2,1,0:T(8,128)(2,1)} %param.7) | copy-start | bytes 7962628
  6.5 128.0 %all-reduce.2.cloned.1.call-start = ((), (), s32[]{:S(2)}) async-start(), calls=%async_computation | async-start | bytes 786432 | tf_op jit(solution)/shard_map/psum | solution.py:82
  10.4 9.9 %collective-permute-start.1 = (f32[192,704]{1,0:T(8,128)S(1)}, f32[192,704]{1,0:T(8,128)S(1)}, u32[]{:S(2)}, u32[]{:S(2)}) collective-permute-start(f32[192,704]{1,0:T(8,128)S(1)} %pad_maximum_fusion.4), channel_id=1, source_target_pairs={{0,3},{1,0},{2,1},{3,2},{4,7},{5,4},{6,5},{7,6},{8,11},{9,8},{10,9... | collective-permute-start | bytes 1622024 | tf_op jit(solution)/shard_map/ppermute | solution.py:13
  13.1 16.9 %collective-permute-start = (f32[192,704]{1,0:T(8,128)S(1)}, f32[192,704]{1,0:T(8,128)S(1)}, u32[]{:S(2)}, u32[]{:S(2)}) collective-permute-start(f32[192,704]{1,0:T(8,128)S(1)} %pad_maximum_fusion.3), channel_id=1, source_target_pairs={{0,28},{4,0},{8,4},{12,8},{16,12},{20,16},{24,20},{28,24},{1,29},{... | collective-permute-start | bytes 1622024 | tf_op jit(solution)/shard_map/ppermute | solution.py:13
  20.3 9.7 %copy-start.7 = (f32[192,704]{1,0:T(8,128)}, f32[192,704]{1,0:T(8,128)S(1)}, u32[]{:S(2)}) copy-start(f32[192,704]{1,0:T(8,128)S(1)} %collective-permute-done.1) | copy-start | bytes 1622020
  30.0 1.3 copy-start.9
  48.6 1.1 copy-start.8
  48.6 1.2 copy-start.10
  49.9 1.4 copy-start.5
  51.3 1.6 %copy-start.12 = (f32[3,192,16]{1,2,0:T(8,128)S(1)}, f32[3,192,16]{1,2,0:T(8,128)}, u32[]{:S(2)}) copy-start(f32[3,192,16]{1,2,0:T(8,128)} %param.8) | copy-start | bytes 110596
  52.5 13.3 %copy-start.1 = (f32[3,192,512]{2,1,0:T(8,128)}, f32[3,192,512]{2,1,0:T(8,128)S(1)}, u32[]{:S(2)}) copy-start(f32[3,192,512]{2,1,0:T(8,128)S(1)} %fusion.10) | copy-start | bytes 3538948
  52.5 13.2 %collective-permute-start.2 = (f32[192,512]{1,0:T(8,128)S(1)}, f32[192,512]{1,0:T(8,128)S(1)}, u32[]{:S(2)}, u32[]{:S(2)}) collective-permute-start(f32[192,512]{1,0:T(8,128)S(1)} %slice_bitcast_fusion.7), channel_id=1, source_target_pairs={{0,4},{4,8},{8,12},{12,16},{16,20},{20,24},{24,28},{28,0},{1,5},{5... | collective-permute-start | bytes 1179656 | tf_op jit(solution)/shard_map/ppermute | solution.py:13
  65.8 34.8 %copy-start.11 = (f32[192,384]{1,0:T(8,128)S(1)}, f32[192,384]{1,0:T(8,128)}, u32[]{:S(2)}) copy-start(f32[192,384]{1,0:T(8,128)} %param.9) | copy-start | bytes 884740
  66.6 1.4 copy-start.4
  68.0 34.2 %collective-permute-start.3 = (f32[192,512]{1,0:T(8,128)}, f32[192,512]{1,0:T(8,128)}, u32[]{:S(2)}, u32[]{:S(2)}) collective-permute-start(f32[192,512]{1,0:T(8,128)} %get-tuple-element.15), channel_id=1, source_target_pairs={{0,1},{1,2},{2,3},{3,0},{4,5},{5,6},{6,7},{7,4},{8,9},{9,10},{10,1... | collective-permute-start | bytes 1179656 | tf_op jit(solution)/shard_map/ppermute | solution.py:13
  104.1 3.9 %copy-start.2 = (f32[1,1,6,192,192]{4,3,2,1,0:T(8,128)S(1)}, f32[1,1,6,192,192]{4,3,2,1,0:T(8,128)}, u32[]{:S(2)}) copy-start(f32[1,1,6,192,192]{4,3,2,1,0:T(8,128)} %param.6) | copy-start | bytes 2654212
  122.8 1.8 %copy-start.3 = (f32[6,192,512]{2,1,0:T(8,128)}, f32[6,192,512]{2,1,0:T(8,128)S(1)}, u32[]{:S(2)}) copy-start(f32[6,192,512]{2,1,0:T(8,128)S(1)} %convolution_bitcast_fusion.1) | copy-start | bytes 7077892
  124.6 11.9 %collective-permute-start.4 = (f32[192,512]{1,0:T(8,128)}, f32[192,512]{1,0:T(8,128)}, u32[]{:S(2)}, u32[]{:S(2)}) collective-permute-start(f32[192,512]{1,0:T(8,128)} %get-tuple-element.7), channel_id=1, source_target_pairs={{0,28},{4,0},{8,4},{12,8},{16,12},{20,16},{24,20},{28,24},{1,29},{... | collective-permute-start | bytes 1179656 | tf_op jit(solution)/shard_map/ppermute | solution.py:13
  126.0 10.6 %collective-permute-start.5 = (f32[192,512]{1,0:T(8,128)}, f32[192,512]{1,0:T(8,128)}, u32[]{:S(2)}, u32[]{:S(2)}) collective-permute-start(f32[192,512]{1,0:T(8,128)} %get-tuple-element.9), channel_id=1, source_target_pairs={{0,3},{1,0},{2,1},{3,2},{4,7},{5,4},{6,5},{7,6},{8,11},{9,8},{10,9... | collective-permute-start | bytes 1179656 | tf_op jit(solution)/shard_map/ppermute | solution.py:13
  136.5 1.6 %copy-start.6 = (f32[1,192,512]{2,1,0:T(8,128)S(1)}, f32[1,192,512]{2,1,0:T(8,128)}, u32[]{:S(2)}) copy-start(f32[1,192,512]{2,1,0:T(8,128)} %get-tuple-element.8) | copy-start | bytes 1179652
Sparse Core Ops, SparseCore 0:
  102.4 32.0 all-reduce.1
where the time goes:
time: 148 us; the launch traced here: 147 us
  matrix products  36.1 us (24%)
  waiting for transfers between devices  33 us (22%)
  blocking collectives  32.6 us (22%)
  between operations  13.8 us (9%)
  local copies, waits for them, and re-layouts  13.2 us (9%)
  other arithmetic  9.77 us (7%)
  starting transfers between devices  8.85 us (6%)
    all_gather x1, blocking collectives, per_device(): lax.all_gather(restricted_residual, 'wide', axis=0, tiled=True)  32.6 us
    ppermute x6, waiting for transfers between devices, passed_along(): return lax.ppermute(value, axis, pairs)  24.5 us
    dot_general x4, matrix products, apply_faces(): jnp.einsum('fij,fjr->fir', blocks, fields, precision=exact_arithmetic_mode)  11.7 us
    dot_general x12, matrix products, newton_schulz(): jnp.einsum('bij,bjk->bik', matrices, approx, precision=exact_arithmetic_m...  8.92 us
    ppermute x6, starting transfers between devices, passed_along(): return lax.ppermute(value, axis, pairs)  8.85 us
    dot_general x12, matrix products, newton_schulz(): jnp.einsum('bij,bjk->bik', approx, product, precision=exact_arithmetic_mode)  8.59 us
    psum x1, waiting for transfers between devices, per_device(): summed = lax.psum(incomplete_total, 'narrow')  8.51 us
    unnamed x29, local copies, waits for them, and re-layouts  6.61 us
  transfers between devices with their start and end apart: 7, of which 4 were waited for; matrix products, arithmetic and copies ran while one was open for 18% of the time, Pallas kernels for 0%

commit v1 on v0

--- a/solution.py
+++ b/solution.py
@@ -5,6 +5,22 @@
 
 NS_STEPS = 12
 exact_arithmetic_mode = lax.Precision.HIGHEST
+
+
+def collect(x, axis, dim):
+    ways, here, step = (lax.axis_size(axis), lax.axis_index(axis), x.shape[dim])
+    shape = [n * ways if d == dim else n for d, n in enumerate(x.shape)]
+    full = lax.dynamic_update_slice_in_dim(jnp.zeros(shape, x.dtype), x, here * step, axis=dim)
+    going_up = going_down = x
+    for far in range(1, ways // 2 + 1):
+        going_up = lax.ppermute(going_up, axis, [(d, (d + 1) % ways) for d in range(ways)])
+        full = lax.dynamic_update_slice_in_dim(full, going_up, (here - far) % ways * step, axis=dim)
+        if 2 * far < ways:
+            going_down = lax.ppermute(going_down, axis, [(d, (d - 1) % ways) for d in range(ways)])
+            full = lax.dynamic_update_slice_in_dim(
+                full, going_down, (here + far) % ways * step, axis=dim
+            )
+    return full
 
 
 def passed_along(value, axis, steps):
@@ -74,7 +90,7 @@
     restricted_residual = restricted_residual.reshape(-1, columns_count)
     incomplete_total = jnp.dot(
         coarse_inverse,
-        lax.all_gather(restricted_residual, "wide", axis=0, tiled=True),
+        collect(restricted_residual, "wide", 0),
         precision=exact_arithmetic_mode,
         preferred_element_type=jnp.float32,
     )

time: 148 us -> 141 us (0.953)
  blocking collectives: 32.6 us -> 0 us
  starting transfers between devices: 8.85 us -> 23.7 us
  waiting for transfers between devices: 33 us -> 40.1 us
  local copies, waits for them, and re-layouts: 13.2 us -> 15.4 us
    all_gather x1 -> x0, blocking collectives: 32.6 us -> none  [per_device(): lax.all_gather(restricted_residual, 'wide', axis=0, tiled=True)]
    ppermute x0 -> x7, waiting for transfers between devices: none -> 19.7 us  [the longest x4 10.2 us: collect(): lax.ppermute(going_up, axis, [(d, (d + 1) % ways) for d in range(ways)])]
    ppermute x0 -> x7, starting transfers between devices: none -> 12 us  [the longest x3 9.95 us: collect(): lax.ppermute(going_down, axis, [(d, (d - 1) % ways) for d in range(ways)])]
    ppermute x6, waiting for transfers between devices: 24.5 us -> 17.2 us  [passed_along(): return lax.ppermute(value, axis, pairs)]
    psum x1, waiting for transfers between devices: 8.51 us -> 3.15 us  [per_device(): summed = lax.psum(incomplete_total, 'narrow')]
    ppermute x6, starting transfers between devices: 8.85 us -> 11.7 us  [passed_along(): return lax.ppermute(value, axis, pairs)]
    dynamic_update_slice x0 -> x8, local copies, waits for them, and re-layouts: none -> 1.99 us  [the longest x1 1.01 us: collect(): lax.dynamic_update_slice_in_dim(jnp.zeros(shape, x.dtype), x, here * step...]
    unnamed x29 -> x33, local copies, waits for them, and re-layouts: 6.61 us -> 6.75 us
  transfers between devices with their start and end apart: 7 -> 14, of which waited for: 4 -> 8; matrix products, arithmetic and copies ran while one was open for 18% -> 35% of each run, Pallas kernels for 0% -> 0%
where the time goes in v1:
time: 141 us; the launch traced here: 140 us
  waiting for transfers between devices  40.1 us (28%)
  matrix products  36.7 us (26%)
  starting transfers between devices  23.7 us (17%)
  local copies, waits for them, and re-layouts  15.4 us (11%)
  between operations  13.9 us (10%)
  other arithmetic  10.7 us (8%)
    ppermute x6, waiting for transfers between devices, passed_along(): return lax.ppermute(value, axis, pairs)  17.2 us
    ppermute x6, starting transfers between devices, passed_along(): return lax.ppermute(value, axis, pairs)  11.7 us
    dot_general x4, matrix products, apply_faces(): jnp.einsum('fij,fjr->fir', blocks, fields, precision=exact_arithmetic_mode)  11.7 us
    ppermute x4, waiting for transfers between devices, collect(): lax.ppermute(going_up, axis, [(d, (d + 1) % ways) for d in range(ways)])  10.2 us
    ppermute x3, starting transfers between devices, collect(): lax.ppermute(going_down, axis, [(d, (d - 1) % ways) for d in range(ways)])  9.95 us
    ppermute x3, waiting for transfers between devices, collect(): lax.ppermute(going_down, axis, [(d, (d - 1) % ways) for d in range(ways)])  9.46 us
    dot_general x12, matrix products, newton_schulz(): jnp.einsum('bij,bjk->bik', matrices, approx, precision=exact_arithmetic_m...  8.94 us
    dot_general x12, matrix products, newton_schulz(): jnp.einsum('bij,bjk->bik', approx, product, precision=exact_arithmetic_mode)  8.57 us
  transfers between devices with their start and end apart: 14, of which 8 were waited for; matrix products, arithmetic and copies ran while one was open for 35% of the time, Pallas kernels for 0%

profile of v1, /device:TPU:0, one launch (start us, length us, event | category | flops | bytes accessed | tf_op | source)
XLA Modules:
  0.0 140.5 jit_solution(12704866786178853494)
XLA Ops:
  6.5 1.4 %add_bitcast_fusion.1 = (f32[1,192,192]{2,1,0:T(8,128)S(1)}, f32[192,192]{1,0:T(8,128)S(1)}, f32[192,192]{1,0:T(8,128)S(1)}) fusion(f32[1,1,6,192,192]{4,3,2,1,0:T(8,128)} %param.6), kind=kLoop, calls=%fused_computation.66 | loop fusion | flops 36864 | bytes 1032192 | tf_op jit(solution)/shard_map/add | solution.py:60
  8.0 1.5 %slice_bitcast_fusion.6 = (f32[192,512]{1,0:T(8,128)S(1)}, f32[192,512]{1,0:T(8,128)S(1)}, f32[1,192,512]{2,1,0:T(8,128)S(1)}) fusion(f32[1,1,6,192,512]{4,3,2,1,0:T(8,128)} %param.5), kind=kLoop, calls=%fused_computation.57 | loop fusion | flops 98304 | bytes 2752512 | tf_op jit(solution)/shard_map/squeeze | solution.py:52
  9.5 1.0 pad_maximum_fusion.4
  10.5 2.4 %collective-permute-start.1 = (f32[192,704]{1,0:T(8,128)}, f32[192,704]{1,0:T(8,128)}, u32[]{:S(2)}, u32[]{:S(2)}) collective-permute-start(f32[192,704]{1,0:T(8,128)} %pad_maximum_fusion.4), channel_id=1, source_target_pairs={{0,3},{1,0},{2,1},{3,2},{4,7},{5,4},{6,5},{7,6},{8,11},{9,8},{10,9... | collective-permute-start | bytes 1622024 | tf_op jit(solution)/shard_map/ppermute | solution.py:29
  12.9 1.0 pad_maximum_fusion.3
  13.9 4.6 %collective-permute-start = (f32[192,704]{1,0:T(8,128)}, f32[192,704]{1,0:T(8,128)}, u32[]{:S(2)}, u32[]{:S(2)}) collective-permute-start(f32[192,704]{1,0:T(8,128)} %pad_maximum_fusion.3), channel_id=1, source_target_pairs={{0,28},{4,0},{8,4},{12,8},{16,12},{20,16},{24,20},{28,24},{1,29},{... | collective-permute-start | bytes 1622024 | tf_op jit(solution)/shard_map/ppermute | solution.py:29
  18.4 2.1 %collective-permute-done.1 = f32[192,704]{1,0:T(8,128)} collective-permute-done((f32[192,704]{1,0:T(8,128)}, f32[192,704]{1,0:T(8,128)}, u32[]{:S(2)}, u32[]{:S(2)}) %collective-permute-start.1) | collective-permute-done | bytes 540704 | tf_op jit(solution)/shard_map/ppermute | solution.py:29
  20.6 10.5 %collective-permute-done = f32[192,704]{1,0:T(8,128)} collective-permute-done((f32[192,704]{1,0:T(8,128)}, f32[192,704]{1,0:T(8,128)}, u32[]{:S(2)}, u32[]{:S(2)}) %collective-permute-start) | collective-permute-done | bytes 540704 | tf_op jit(solution)/shard_map/ppermute | solution.py:29
  31.1 1.7 %fusion.19 = (f32[1,192,512]{2,1,0:T(8,128)S(1)}, f32[1,192,512]{2,1,0:T(8,128)S(1)}) fusion(f32[192,704]{1,0:T(8,128)} %collective-permute-done, f32[1,1,6,192,512]{4,3,2,1,0:T(8,128)} %param.5, f32[192,704]{1,0:T(8,128)} %collective-permute-done.1), kind=kLoop, calls=%fused_computation.52 | loop fusion | flops 196608 | bytes 2359296 | tf_op jit(solution)/shard_map/stack | solution.py:64
  32.8 1.4 fusion.9
  34.2 5.2 %collective-permute-start.7 = (f32[48,512]{1,0:T(8,128)}, f32[48,512]{1,0:T(8,128)}, u32[]{:S(2)}, u32[]{:S(2)}) collective-permute-start(f32[48,512]{1,0:T(8,128)} %bitcast.32), channel_id=1, source_target_pairs={{0,28},{4,0},{8,4},{12,8},{16,12},{20,16},{24,20},{28,24},{1,29},{... | collective-permute-start | bytes 294920 | tf_op jit(solution)/shard_map/ppermute | solution.py:19
  39.4 1.3 fusion.23
  41.0 0.8 fusion.11
  41.8 0.8 convolution_subtract_fusion.11
  45.5 0.7 fusion.35
  46.9 0.7 fusion.34
  48.4 0.7 fusion.33
  49.8 0.7 fusion.32
  51.3 0.7 fusion.31
  52.7 0.9 fusion.30
  59.2 1.2 fusion.10
  60.6 1.0 constant_dynamic-update-slice_fusion.7
  61.6 4.8 %collective-permute-start.9 = (f32[48,512]{1,0:T(8,128)}, f32[48,512]{1,0:T(8,128)S(1)}, u32[]{:S(2)}, u32[]{:S(2)}) collective-permute-start(f32[48,512]{1,0:T(8,128)} %collective-permute-done.7), channel_id=1, source_target_pairs={{0,28},{4,0},{8,4},{12,8},{16,12},{20,16},{24,20},{28,24},{1,29},{... | collective-permute-start | bytes 294920 | tf_op jit(solution)/shard_map/ppermute | solution.py:19
  66.4 0.9 constant_dynamic-update-slice_fusion.5
  67.3 9.5 %collective-permute-done.9 = f32[48,512]{1,0:T(8,128)S(1)} collective-permute-done((f32[48,512]{1,0:T(8,128)}, f32[48,512]{1,0:T(8,128)S(1)}, u32[]{:S(2)}, u32[]{:S(2)}) %collective-permute-start.9) | collective-permute-done | bytes 98336 | tf_op jit(solution)/shard_map/ppermute | solution.py:19
  76.8 2.0 %collective-permute-start.10 = (f32[48,512]{1,0:T(8,128)S(1)}, f32[48,512]{1,0:T(8,128)S(1)}, u32[]{:S(2)}, u32[]{:S(2)}) collective-permute-start(f32[48,512]{1,0:T(8,128)S(1)} %collective-permute-done.8), channel_id=1, source_target_pairs={{0,4},{4,8},{8,12},{12,16},{16,20},{20,24},{24,28},{28,0},{1,5},{5... | collective-permute-start | bytes 294920 | tf_op jit(solution)/shard_map/ppermute | solution.py:16
  78.8 5.3 %collective-permute-done.10 = f32[48,512]{1,0:T(8,128)S(1)} collective-permute-done((f32[48,512]{1,0:T(8,128)S(1)}, f32[48,512]{1,0:T(8,128)S(1)}, u32[]{:S(2)}, u32[]{:S(2)}) %collective-permute-start.10) | collective-permute-done | bytes 98336 | tf_op jit(solution)/shard_map/ppermute | solution.py:16
  84.2 0.8 slice_bitcast_fusion.4
  85.0 1.4 %copy-done.4 = f32[6,192,512]{2,1,0:T(8,128)} copy-done((f32[6,192,512]{2,1,0:T(8,128)}, f32[6,192,512]{2,1,0:T(8,128)S(1)}, u32[]{:S(2)}) %copy-start.4) | copy-done | bytes 2359320
  86.4 5.0 %collective-permute-done.12 = f32[48,512]{1,0:T(8,128)S(1)} collective-permute-done((f32[48,512]{1,0:T(8,128)S(1)}, f32[48,512]{1,0:T(8,128)S(1)}, u32[]{:S(2)}, u32[]{:S(2)}) %collective-permute-start.12) | collective-permute-done | bytes 98336 | tf_op jit(solution)/shard_map/ppermute | solution.py:16
  91.4 1.6 %convolution_bitcast_fusion.3 = f32[192,512]{1,0:T(8,128)} fusion(f32[384,512]{1,0:T(8,128)S(1)} %constant_dynamic-update-slice_fusion, f32[192,384]{1,0:T(8,128)S(1)} %copy-done.12), kind=kOutput, calls=%fused_computation.19 | convolution fusion | flops 452984832 | bytes 1474560 | tf_op jit(solution)/shard_map/dot_general | solution.py:91
  93.1 0.9 collective-permute-done.3
  93.9 1.8 %bitcast_dynamic-update-slice_fusion = f32[6,192,512]{2,1,0:T(8,128)} fusion(f32[6,192,512]{2,1,0:T(8,128)} %copy-done.4, f32[192,512]{1,0:T(8,128)} %collective-permute-done.3), kind=kLoop, calls=%fused_computation.53 | loop fusion | bytes 786432
  95.7 2.2 %slice_dynamic-update-slice_fusion = f32[6,192,512]{2,1,0:T(8,128)} fusion(f32[6,192,512]{2,1,0:T(8,128)} %bitcast_dynamic-update-slice_fusion, f32[3,192,512]{2,1,0:T(8,128)} %copy-done.1), kind=kLoop, calls=%fused_computation.30 | loop fusion | bytes 1572864
  97.9 1.8 %slice_dynamic-update-slice_fusion.1 = f32[6,192,512]{2,1,0:T(8,128)} fusion(f32[6,192,512]{2,1,0:T(8,128)} %slice_dynamic-update-slice_fusion, f32[3,192,512]{2,1,0:T(8,128)} %copy-done.1), kind=kLoop, calls=%fused_computation.47 | loop fusion | bytes 786432 | tf_op jit(solution)/shard_map/stack | solution.py:76
  99.7 4.0 %convolution_convert_fusion = bf16[6,512,192]{1,2,0:T(8,128)(2,1)S(1)} fusion(f32[6,192,512]{2,1,0:T(8,128)} %slice_dynamic-update-slice_fusion.1, f32[1,1,6,192,192]{4,3,2,1,0:T(8,128)S(1)} %copy-done.2), kind=kOutput, calls=%fused_computation.3 | convolution fusion | flops 1359544320 | bytes 4423680 | tf_op jit(solution)/shard_map/fij,fjr->fir/dot_general | solution.py:44
  103.7 3.4 %convolution_bitcast_fusion = f32[1152,512]{0,1:T(8,128)} fusion(bf16[1152,512]{1,0:T(8,128)(2,1)S(1)} %bitcast.127, bf16[1,1,1152,1152]{3,2,1,0:T(8,128)(2,1)S(1)} %copy-done), kind=kOutput, calls=%fused_computation | convolution fusion | flops 1358954496 | bytes 6193152 | tf_op jit(solution)/shard_map/dot_general | solution.py:102
  107.1 3.1 %copy.8 = f32[1152,512]{1,0:T(8,128)} copy(f32[1152,512]{0,1:T(8,128)} %convolution_bitcast_fusion) | data formatting | bytes 4718592 | tf_op jit(solution)/shard_map/dot_general | solution.py:102
  110.2 4.3 %convolution_bitcast_fusion.1 = f32[6,192,512]{2,1,0:T(8,128)S(1)} fusion(f32[6,192,512]{2,1,0:T(8,128)} %bitcast.126, f32[1,1,6,192,192]{4,3,2,1,0:T(8,128)} %param.6), kind=kOutput, calls=%fused_computation.2 | convolution fusion | flops 1358954496 | bytes 5603328 | tf_op jit(solution)/shard_map/fij,fjr->fir/dot_general | solution.py:44
  114.5 1.1 slice_bitcast_fusion.2
  115.6 0.7 copy-done.3
  116.3 4.7 %collective-permute-start.4 = (f32[192,512]{1,0:T(8,128)}, f32[192,512]{1,0:T(8,128)}, u32[]{:S(2)}, u32[]{:S(2)}) collective-permute-start(f32[192,512]{1,0:T(8,128)} %get-tuple-element.7), channel_id=1, source_target_pairs={{0,28},{4,0},{8,4},{12,8},{16,12},{20,16},{24,20},{28,24},{1,29},{... | collective-permute-start | bytes 1179656 | tf_op jit(solution)/shard_map/ppermute | solution.py:29
  121.0 3.1 %all-reduce.2.cloned.1.call-done = f32[192,512]{1,0:T(8,128)} async-done(((f32[192,512]{1,0:T(8,128)}), f32[192,512]{1,0:T(8,128)}) %all-reduce.2.cloned.1.call-update) | async-done | bytes 393232 | tf_op jit(solution)/shard_map/psum | solution.py:98
  124.2 0.9 constant_dynamic-slice_fusion
  125.1 1.1 convolution_bitcast_fusion.2
  126.2 3.7 %collective-permute-done.4 = f32[192,512]{1,0:T(8,128)} collective-permute-done((f32[192,512]{1,0:T(8,128)}, f32[192,512]{1,0:T(8,128)}, u32[]{:S(2)}, u32[]{:S(2)}) %collective-permute-start.4) | collective-permute-done | bytes 393248 | tf_op jit(solution)/shard_map/ppermute | solution.py:29
  129.9 1.5 %fusion.17 = (f32[1,192,512]{2,1,0:T(8,128)S(1)}, f32[1,192,512]{2,1,0:T(8,128)S(1)}) fusion(f32[192,512]{1,0:T(8,128)} %collective-permute-done.4, f32[6,192,512]{2,1,0:T(8,128)} %copy-done.3, f32[192,512]{1,0:T(8,128)} %collective-permute-done.5), kind=kLoop, calls=%fused_computation.46 | loop fusion | flops 196608 | bytes 2359296 | tf_op jit(solution)/shard_map/stack | solution.py:107
  131.4 2.2 %fusion.1 = f32[1,1,3,192,512]{4,3,2,1,0:T(8,128)} fusion(f32[3,192,512]{2,1,0:T(8,128)S(1)} %convolution_bitcast_fusion.2, f32[3,192,192]{2,1,0:T(8,128)S(1)} %convolution_subtract_fusion, f32[1,192,512]{2,1,0:T(8,128)S(1)} %copy-done.11, f32[1,192,512]{2,1,0:T(8,128)S(1)} %get-tuple-element.6, f32[1,192,512]{2,1,0:T(8,128)S(1)} %get-tuple-element.5), kind=kOutput, calls=%fused_computation.6 | convolution fusion | flops 680361984 | bytes 3981312 | tf_op jit(solution)/shard_map/fij,fjr->fir/dot_general | solution.py:44
  (71 shorter events, 12.6 us)
Async XLA Ops:
  6.5 97.1 %copy-start = (bf16[1,1,1152,1152]{3,2,1,0:T(8,128)(2,1)S(1)}, bf16[1,1,1152,1152]{3,2,1,0:T(8,128)(2,1)}, u32[]{:S(2)}) copy-start(bf16[1,1,1152,1152]{3,2,1,0:T(8,128)(2,1)} %param.7) | copy-start | bytes 7962628
  6.5 117.6 %all-reduce.2.cloned.1.call-start = ((), (), s32[]{:S(2)}) async-start(), calls=%async_computation | async-start | bytes 786432 | tf_op jit(solution)/shard_map/psum | solution.py:98
  9.5 23.4 %copy-start.9 = (f32[1,192,512]{2,1,0:T(8,128)}, f32[1,192,512]{2,1,0:T(8,128)S(1)}, u32[]{:S(2)}) copy-start(f32[1,192,512]{2,1,0:T(8,128)S(1)} %get-tuple-element.14) | copy-start | bytes 1179652
  10.5 10.1 %collective-permute-start.1 = (f32[192,704]{1,0:T(8,128)}, f32[192,704]{1,0:T(8,128)}, u32[]{:S(2)}, u32[]{:S(2)}) collective-permute-start(f32[192,704]{1,0:T(8,128)} %pad_maximum_fusion.4), channel_id=1, source_target_pairs={{0,3},{1,0},{2,1},{3,2},{4,7},{5,4},{6,5},{7,6},{8,11},{9,8},{10,9... | collective-permute-start | bytes 1622024 | tf_op jit(solution)/shard_map/ppermute | solution.py:29
  13.9 17.2 %collective-permute-start = (f32[192,704]{1,0:T(8,128)}, f32[192,704]{1,0:T(8,128)}, u32[]{:S(2)}, u32[]{:S(2)}) collective-permute-start(f32[192,704]{1,0:T(8,128)} %pad_maximum_fusion.3), channel_id=1, source_target_pairs={{0,28},{4,0},{8,4},{12,8},{16,12},{20,16},{24,20},{28,24},{1,29},{... | collective-permute-start | bytes 1622024 | tf_op jit(solution)/shard_map/ppermute | solution.py:29
  18.4 14.4 %copy-start.13 = (f32[3,192,16]{1,2,0:T(8,128)S(1)}, f32[3,192,16]{1,2,0:T(8,128)}, u32[]{:S(2)}) copy-start(f32[3,192,16]{1,2,0:T(8,128)} %param.8) | copy-start | bytes 110596
  32.8 7.9 %copy-start.5 = (f32[1,192,512]{2,1,0:T(8,128)}, f32[1,192,512]{2,1,0:T(8,128)S(1)}, u32[]{:S(2)}) copy-start(f32[1,192,512]{2,1,0:T(8,128)S(1)} %get-tuple-element.10) | copy-start | bytes 1179652
  32.8 7.9 %copy-start.7 = (f32[1,192,512]{2,1,0:T(8,128)}, f32[1,192,512]{2,1,0:T(8,128)S(1)}, u32[]{:S(2)}) copy-start(f32[1,192,512]{2,1,0:T(8,128)S(1)} %get-tuple-element.11) | copy-start | bytes 1179652
  34.2 27.4 %collective-permute-start.7 = (f32[48,512]{1,0:T(8,128)}, f32[48,512]{1,0:T(8,128)}, u32[]{:S(2)}, u32[]{:S(2)}) collective-permute-start(f32[48,512]{1,0:T(8,128)} %bitcast.32), channel_id=1, source_target_pairs={{0,28},{4,0},{8,4},{12,8},{16,12},{20,16},{24,20},{28,24},{1,29},{... | collective-permute-start | bytes 294920 | tf_op jit(solution)/shard_map/ppermute | solution.py:19
  39.4 27.0 %collective-permute-start.6 = (f32[48,512]{1,0:T(8,128)}, f32[48,512]{1,0:T(8,128)S(1)}, u32[]{:S(2)}, u32[]{:S(2)}) collective-permute-start(f32[48,512]{1,0:T(8,128)} %bitcast.32), channel_id=1, source_target_pairs={{0,4},{4,8},{8,12},{12,16},{16,20},{20,24},{24,28},{28,0},{1,5},{5... | collective-permute-start | bytes 294920 | tf_op jit(solution)/shard_map/ppermute | solution.py:16
  58.0 1.0 copy-start.6
  58.0 1.1 copy-start.8
  58.0 1.2 copy-start.10
  60.4 23.8 %copy-start.1 = (f32[3,192,512]{2,1,0:T(8,128)}, f32[3,192,512]{2,1,0:T(8,128)S(1)}, u32[]{:S(2)}) copy-start(f32[3,192,512]{2,1,0:T(8,128)S(1)} %fusion.10) | copy-start | bytes 3538948
  60.4 23.7 %collective-permute-start.2 = (f32[192,512]{1,0:T(8,128)S(1)}, f32[192,512]{1,0:T(8,128)S(1)}, u32[]{:S(2)}, u32[]{:S(2)}) collective-permute-start(f32[192,512]{1,0:T(8,128)S(1)} %slice_bitcast_fusion.7), channel_id=1, source_target_pairs={{0,4},{4,8},{8,12},{12,16},{16,20},{20,24},{24,28},{28,0},{1,5},{5... | collective-permute-start | bytes 1179656 | tf_op jit(solution)/shard_map/ppermute | solution.py:29
  61.6 15.2 %collective-permute-start.9 = (f32[48,512]{1,0:T(8,128)}, f32[48,512]{1,0:T(8,128)S(1)}, u32[]{:S(2)}, u32[]{:S(2)}) collective-permute-start(f32[48,512]{1,0:T(8,128)} %collective-permute-done.7), channel_id=1, source_target_pairs={{0,28},{4,0},{8,4},{12,8},{16,12},{20,16},{24,20},{28,24},{1,29},{... | collective-permute-start | bytes 294920 | tf_op jit(solution)/shard_map/ppermute | solution.py:19
  66.4 10.4 %collective-permute-start.8 = (f32[48,512]{1,0:T(8,128)S(1)}, f32[48,512]{1,0:T(8,128)S(1)}, u32[]{:S(2)}, u32[]{:S(2)}) collective-permute-start(f32[48,512]{1,0:T(8,128)S(1)} %collective-permute-done.6), channel_id=1, source_target_pairs={{0,4},{4,8},{8,12},{12,16},{16,20},{20,24},{24,28},{28,0},{1,5},{5... | collective-permute-start | bytes 294920 | tf_op jit(solution)/shard_map/ppermute | solution.py:16
  76.8 9.6 %collective-permute-start.11 = (f32[48,512]{1,0:T(8,128)S(1)}, f32[48,512]{1,0:T(8,128)S(1)}, u32[]{:S(2)}, u32[]{:S(2)}) collective-permute-start(f32[48,512]{1,0:T(8,128)S(1)} %collective-permute-done.9), channel_id=1, source_target_pairs={{0,28},{4,0},{8,4},{12,8},{16,12},{20,16},{24,20},{28,24},{1,29},{... | collective-permute-start | bytes 294920 | tf_op jit(solution)/shard_map/ppermute | solution.py:19
  76.8 7.3 %collective-permute-start.10 = (f32[48,512]{1,0:T(8,128)S(1)}, f32[48,512]{1,0:T(8,128)S(1)}, u32[]{:S(2)}, u32[]{:S(2)}) collective-permute-start(f32[48,512]{1,0:T(8,128)S(1)} %collective-permute-done.8), channel_id=1, source_target_pairs={{0,4},{4,8},{8,12},{12,16},{16,20},{20,24},{24,28},{28,0},{1,5},{5... | collective-permute-start | bytes 294920 | tf_op jit(solution)/shard_map/ppermute | solution.py:16
  84.1 7.3 %collective-permute-start.12 = (f32[48,512]{1,0:T(8,128)S(1)}, f32[48,512]{1,0:T(8,128)S(1)}, u32[]{:S(2)}, u32[]{:S(2)}) collective-permute-start(f32[48,512]{1,0:T(8,128)S(1)} %collective-permute-done.10), channel_id=1, source_target_pairs={{0,4},{4,8},{8,12},{12,16},{16,20},{20,24},{24,28},{28,0},{1,5},{5... | collective-permute-start | bytes 294920 | tf_op jit(solution)/shard_map/ppermute | solution.py:16
  84.1 7.3 %copy-start.12 = (f32[192,384]{1,0:T(8,128)S(1)}, f32[192,384]{1,0:T(8,128)}, u32[]{:S(2)}) copy-start(f32[192,384]{1,0:T(8,128)} %param.9) | copy-start | bytes 884740
  85.0 1.4 %copy-start.4 = (f32[6,192,512]{2,1,0:T(8,128)}, f32[6,192,512]{2,1,0:T(8,128)S(1)}, u32[]{:S(2)}) copy-start(f32[6,192,512]{2,1,0:T(8,128)S(1)} %get-tuple-element.16) | copy-start | bytes 7077892
  86.4 7.5 %collective-permute-start.3 = (f32[192,512]{1,0:T(8,128)}, f32[192,512]{1,0:T(8,128)}, u32[]{:S(2)}, u32[]{:S(2)}) collective-permute-start(f32[192,512]{1,0:T(8,128)} %get-tuple-element.15), channel_id=1, source_target_pairs={{0,1},{1,2},{2,3},{3,0},{4,5},{5,6},{6,7},{7,4},{8,9},{9,10},{10,1... | collective-permute-start | bytes 1179656 | tf_op jit(solution)/shard_map/ppermute | solution.py:29
  95.7 4.0 %copy-start.2 = (f32[1,1,6,192,192]{4,3,2,1,0:T(8,128)S(1)}, f32[1,1,6,192,192]{4,3,2,1,0:T(8,128)}, u32[]{:S(2)}) copy-start(f32[1,1,6,192,192]{4,3,2,1,0:T(8,128)} %param.6) | copy-start | bytes 2654212
  114.5 1.8 %copy-start.3 = (f32[6,192,512]{2,1,0:T(8,128)}, f32[6,192,512]{2,1,0:T(8,128)S(1)}, u32[]{:S(2)}) copy-start(f32[6,192,512]{2,1,0:T(8,128)S(1)} %convolution_bitcast_fusion.1) | copy-start | bytes 7077892
  114.5 10.6 %copy-start.14 = (f32[3,192,16]{1,2,0:T(8,128)S(1)}, f32[3,192,16]{1,2,0:T(8,128)}, u32[]{:S(2)}) copy-start(f32[3,192,16]{1,2,0:T(8,128)} %param.8) | copy-start | bytes 110596
  116.3 13.6 %collective-permute-start.4 = (f32[192,512]{1,0:T(8,128)}, f32[192,512]{1,0:T(8,128)}, u32[]{:S(2)}, u32[]{:S(2)}) collective-permute-start(f32[192,512]{1,0:T(8,128)} %get-tuple-element.7), channel_id=1, source_target_pairs={{0,28},{4,0},{8,4},{12,8},{16,12},{20,16},{24,20},{28,24},{1,29},{... | collective-permute-start | bytes 1179656 | tf_op jit(solution)/shard_map/ppermute | solution.py:29
  121.0 8.9 %collective-permute-start.5 = (f32[192,512]{1,0:T(8,128)}, f32[192,512]{1,0:T(8,128)}, u32[]{:S(2)}, u32[]{:S(2)}) collective-permute-start(f32[192,512]{1,0:T(8,128)} %get-tuple-element.9), channel_id=1, source_target_pairs={{0,3},{1,0},{2,1},{3,2},{4,7},{5,4},{6,5},{7,6},{8,11},{9,8},{10,9... | collective-permute-start | bytes 1179656 | tf_op jit(solution)/shard_map/ppermute | solution.py:29
  126.2 5.2 %copy-start.11 = (f32[1,192,512]{2,1,0:T(8,128)S(1)}, f32[1,192,512]{2,1,0:T(8,128)}, u32[]{:S(2)}) copy-start(f32[1,192,512]{2,1,0:T(8,128)} %get-tuple-element.8) | copy-start | bytes 1179652
Sparse Core Ops, SparseCore 0:
  93.2 30.9 all-reduce.1
